TPU v7x, 128 devices: a whole 4x4x4 slice. The times are simulated.
128 devices in a mesh: frame: 4 (over x), pix: 32 (over y, z, core).
Axes of the slice: x: 4, y: 4, z: 4, core: 2. Of those that a mesh axis runs over, the one named last changes fastest.
Arguments:
- frames: bfloat16 [128, 4, 512, 512], P('frame', None, 'pix'), may hold values from -26 to 26
- prev_fg: bfloat16 [128, 4, 512, 512], P('frame', None, 'pix'), may hold values from -3 to 3
- depth_valid: int32 [128, 512, 512], P('frame', 'pix'), may hold values 0 or 1
- sketch: float32 [128, 64], replicated, may hold values from -0.5 to 0.5
- tv_weight: float32 [4], replicated, may hold values from 0.1 to 1
Outputs:
- background: bfloat16 [128, 4, 512, 512], P('frame', None, 'pix')
- foreground: bfloat16 [128, 4, 512, 512], P('frame', None, 'pix')
All inputs are finite; a program needn't handle non-finite values. No bound on the sum of `depth_valid` on one device may be relied on, other than what follows from the above.
Results may differ from a plain program's by a relative error of at most 0.012.
The roundings to bfloat16 on the way count: a program that leaves them out, or rounds other values in their place, can miss the bound.
Values may be sent and summed in bfloat16 or wider, within the bound.
A program may use at most 64 MiB of HBM per device.

v0:
```python
import jax
import jax.numpy as jnp
from jax import lax
from jax.sharding import PartitionSpec as P

POWER = 3
NSWEEP = 5
STEP_SIZE = 0.125


def shortened(shard):

    def short(part):
        return part.astype(jnp.bfloat16) if part.dtype == jnp.float32 else part

    return jax.tree.map(short, shard)


def from_behind(value, axis, steps):
    count = lax.axis_size(axis)
    leading, last = (max(0, -steps), min(count, count - steps))
    return lax.ppermute(value, axis, [(source, source + steps) for source in range(leading, last)])


def exact_dot(left, right):
    return jnp.dot(left, right, precision=lax.Precision.HIGHEST)


def mixing_matrix(gram, sketch):
    basis = sketch
    for turn in range(POWER):
        image = exact_dot(gram, basis)
        factor = jnp.linalg.cholesky(exact_dot(basis.T, image))
        basis = lax.linalg.triangular_solve(
            factor, image, left_side=False, lower=True, transpose_a=True
        )
    image = exact_dot(gram, basis)
    factor = jnp.linalg.cholesky(exact_dot(basis.T, image))
    middle = lax.linalg.triangular_solve(
        factor, exact_dot(basis.T, gram), left_side=True, lower=True
    )
    coeffs = lax.linalg.triangular_solve(
        factor, middle, left_side=True, lower=True, transpose_a=True
    )
    return exact_dot(basis, coeffs)


def pair_rows(left, right):
    return lax.dot_general(
        left, right, (((1,), (1,)), ((), ())), preferred_element_type=jnp.float32
    )


def over_frames(weights, pixels):
    return lax.dot_general(
        weights, pixels, (((0,), (0,)), ((), ())), preferred_element_type=jnp.float32
    )


def dual_update(first, second, down, across, step):
    size = jnp.sqrt(down * down + across * across)
    scale = 1.0 + step * size
    return ((first - step * down) / scale, (second - step * across) / scale)


def col_prev(field):
    return jnp.pad(field[:, :, :, :-1], ((0, 0), (0, 0), (0, 0), (1, 0)))


def col_grad(smooth, last_col):
    next_cols = jnp.pad(smooth[:, :, :, 1:], ((0, 0), (0, 0), (0, 0), (0, 1)))
    return jnp.where(last_col, 0.0, next_cols - smooth)


def local(frames, prev_fg, depth_valid, sketch, tv_weight):
    count, chans, rows, cols = frames.shape
    height = rows * lax.axis_size("pix")
    nval = chans * height * cols
    start_frame = lax.axis_index("frame") * count
    chan_ids = lax.broadcasted_iota(jnp.int32, (1, chans, 1, 1), 1)
    depth_ok = depth_valid[:, None, :, :].astype(jnp.float32)
    valid = jnp.where(chan_ids == chans - 1, depth_ok, jnp.float32(1.0))
    resid = ((frames.astype(jnp.float32) - prev_fg.astype(jnp.float32)) * valid).astype(
        jnp.bfloat16
    )
    flat = resid.reshape(count, chans * rows * cols)
    everyone = lax.all_gather(flat, "frame", axis=0, tiled=True)
    block = pair_rows(everyone, flat)
    summed = lax.psum(block, "pix")
    gram = lax.all_gather(summed, "frame", axis=1, tiled=True)
    gram = gram / nval
    mixing = mixing_matrix(gram, sketch)
    mine = lax.dynamic_slice_in_dim(mixing, start_frame, count, 1).astype(jnp.bfloat16)
    back = over_frames(mine, everyone)
    background = back.reshape(count, chans, rows, cols).astype(jnp.bfloat16)
    rounded = lax.optimization_barrier(background).astype(jnp.float32)
    source = (frames.astype(jnp.float32) - rounded) * valid
    lam = tv_weight.reshape(1, chans, 1, 1)
    step = STEP_SIZE / lam
    last_col = lax.broadcasted_iota(jnp.int32, (1, 1, 1, cols), 3) == cols - 1
    row_ids = lax.axis_index("pix") * rows + lax.broadcasted_iota(jnp.int32, (1, 1, rows, 1), 2)
    last_row = row_ids == height - 1

    def divergence(first, second):
        above = from_behind(shortened(first[:, :, -1:, :]), "pix", 1)
        prev_rows = jnp.concatenate([above, first[:, :, :-1, :]], axis=2)
        return first - prev_rows + (second - col_prev(second))

    first = jnp.zeros_like(source)
    second = jnp.zeros_like(source)
    for sweep in range(NSWEEP):
        smooth = source - lam * divergence(first, second)
        below = from_behind(shortened(smooth[:, :, :1, :]), "pix", -1)
        next_rows = jnp.concatenate([smooth[:, :, 1:, :], below], axis=2)
        down = jnp.where(last_row, 0.0, next_rows - smooth)
        across = col_grad(smooth, last_col)
        first, second = dual_update(first, second, down, across, step)
    smooth = source - lam * divergence(first, second)
    return (background, smooth.astype(jnp.bfloat16))


def solution(mesh):
    placed = (
        P("frame", None, "pix", None),
        P("frame", None, "pix", None),
        P("frame", "pix", None),
        P(),
        P(),
    )
    return jax.shard_map(
        local,
        mesh=mesh,
        in_specs=placed,
        out_specs=(P("frame", None, "pix", None), P("frame", None, "pix", None)),
        check_vma=False,
    )
```

profile of v0, /device:TPU:8, one launch (start us, length us, event | category | flops | bytes accessed | tf_op | source)
XLA Modules:
  0.0 442.0 jit_solution(11430136703876754686)
XLA Ops:
  7.3 1.5 convert_element_type.88
  9.7 3.6 fusion
  13.3 1.5 copy.30
  14.9 0.7 convert_element_type.94
  15.5 1.9 collective-permute-start
  17.5 82.8 %all-gather.2.cloned.1.call-done = bf16[128,32768]{1,0:T(8,128)(2,1)} async-done(((bf16[32,32768]{1,0:T(8,128)(2,1)}), bf16[128,32768]{1,0:T(8,128)(2,1)}) %all-gather.2.cloned.1.call-update) | async-done | bytes 8388624 | tf_op jit(solution)/shard_map/all_gather | solution.py:87
  100.3 6.9 %fusion.61 = f32[128,32]{0,1:T(8,128)S(1)} fusion(bf16[128,32768]{1,0:T(8,128)(2,1)} %all-gather.2.cloned.1.call-done, bf16[32,32768]{1,0:T(8,128)(2,1)} %bitcast.91), kind=kOutput, calls=%fused_computation.132 | convolution fusion | flops 268435456 | bytes 10502144 | tf_op jit(solution)/shard_map/dot_general | solution.py:49
  107.2 110.5 %psum.7 = f32[128,32]{0,1:T(8,128)S(1)} all-reduce(f32[128,32]{0,1:T(8,128)S(1)} %fusion.61), channel_id=1, replica_groups=mesh['frame'=4,'pix'=32] {'pix'}, use_global_device_ids=true, to_apply=%region_0.1 | all-reduce | flops 4096 | bytes 32768 | tf_op jit(solution)/shard_map/psum | solution.py:89
  217.7 12.0 %all_gather.7 = f32[128,128]{0,1:T(8,128)S(1)} all-gather(f32[128,32]{0,1:T(8,128)S(1)} %psum.7), channel_id=1, replica_groups=mesh['frame'=4,'pix'=32] {'frame'}, dimensions={1}, use_global_device_ids=true | all-gather | bytes 81920 | tf_op jit(solution)/shard_map/all_gather | solution.py:90
  230.2 5.8 %cholesky.74 = f32[64,64]{1,0:T(8,128)S(1)} custom-call(f32[64,64]{1,0:T(8,128)S(1)} %add_multiply_fusion), custom_call_target="Cholesky" | custom-call | tf_op jit(solution)/shard_map/jit(cholesky)/cholesky | solution.py:33
  236.7 0.7 fusion.32
  237.4 4.9 %custom-call.13 = f32[1,64,64]{1,2,0:T(8,128)S(1)} custom-call(f32[1,64,64]{2,1,0:T(8,128)S(1)} %fusion.32), custom_call_target="InvertDiagBlocksLowerTriangular" | custom-call | tf_op jit(solution)/shard_map/triangular_solve/custom-call.0 | solution.py:34
  243.0 5.8 %cholesky.85 = f32[64,64]{1,0:T(8,128)S(1)} custom-call(f32[64,64]{1,0:T(8,128)S(1)} %fusion.44), custom_call_target="Cholesky" | custom-call | tf_op jit(solution)/shard_map/jit(cholesky)/cholesky | solution.py:33
  250.2 4.9 %custom-call.14 = f32[1,64,64]{1,2,0:T(8,128)S(1)} custom-call(f32[1,64,64]{2,1,0:T(8,128)S(1)} %fusion.33), custom_call_target="InvertDiagBlocksLowerTriangular" | custom-call | tf_op jit(solution)/shard_map/triangular_solve/custom-call.0 | solution.py:34
  255.8 5.8 %cholesky.96 = f32[64,64]{1,0:T(8,128)S(1)} custom-call(f32[64,64]{1,0:T(8,128)S(1)} %fusion.42), custom_call_target="Cholesky" | custom-call | tf_op jit(solution)/shard_map/jit(cholesky)/cholesky | solution.py:33
  263.0 4.9 %custom-call.15 = f32[1,64,64]{1,2,0:T(8,128)S(1)} custom-call(f32[1,64,64]{2,1,0:T(8,128)S(1)} %fusion.34), custom_call_target="InvertDiagBlocksLowerTriangular" | custom-call | tf_op jit(solution)/shard_map/triangular_solve/custom-call.0 | solution.py:34
  268.9 5.8 %cholesky.107 = f32[64,64]{1,0:T(8,128)S(1)} custom-call(f32[64,64]{1,0:T(8,128)S(1)} %fusion.40), custom_call_target="Cholesky" | custom-call | tf_op jit(solution)/shard_map/jit(cholesky)/cholesky | solution.py:38
  276.1 4.9 %custom-call.10 = f32[1,64,64]{1,2,0:T(8,128)S(1)} custom-call(f32[1,64,64]{2,1,0:T(8,128)S(1)} %fusion.35), custom_call_target="InvertDiagBlocksLowerTriangular" | custom-call | tf_op jit(solution)/shard_map/triangular_solve | solution.py:42
  281.7 4.6 %convolution_convert_fusion = bf16[32,32768]{1,0:T(8,128)(2,1)S(1)} fusion(bf16[128,32768]{1,0:T(8,128)(2,1)} %all-gather.2.cloned.1.call-done, bf16[128,128]{0,1:T(8,128)(2,1)S(1)} %fusion.66, s32[]{:T(128)S(6)} %select_n.43), kind=kOutput, calls=%fused_computation | convolution fusion | flops 269484032 | bytes 10493956 | tf_op jit(solution)/shard_map/dot_general | solution.py:55
  286.3 0.7 copy.31
  287.1 3.5 multiply_subtract_fusion
  290.6 1.9 copy-done.5
  292.5 1.9 collective-permute-start.1
  294.4 2.2 copy-done.6
  296.6 1.1 slice.151
  297.8 0.9 slice-done
  298.7 3.6 subtract_divide_fusion.8
  302.4 2.5 collective-permute-start.2
  304.9 0.7 slice.153
  305.6 7.1 %collective-permute-done.2 = bf16[32,4,1,512]{3,0,2,1:T(8,128)(2,1)S(1)} collective-permute-done((bf16[32,4,1,512]{3,0,2,1:T(8,128)(2,1)S(1)}, bf16[32,4,1,512]{3,0,2,1:T(8,128)(2,1)S(1)}, u32[]{:S(2)}, u32[]{:S(2)}) %collective-permute-start.2) | collective-permute-done | bytes 131104 | tf_op jit(solution)/shard_map/ppermute | solution.py:22
  312.8 5.2 %fusion.4 = f32[32,4,16,512]{3,0,2,1:T(8,128)S(1)} fusion(f32[32,4,16,512]{3,0,2,1:T(8,128)S(1)} %get-tuple-element.17, f32[32,4,15,512]{3,0,2,1:T(8,128)S(1)} %slice.153, f32[32,4,1,512]{3,0,2,1:T(8,128)S(1)} %convert_element_type.96, f32[32,4,16,512]{3,0,2,1:T(8,128)S(1)} %get-tuple-element.16, f32[32,4,16,511]{3,0,2,1:T(8,128)S(1)} %bitcast.88, ...), kind=kLoop, calls=%fused_computation.11 | loop fusion | flops 11534336 | bytes 26206228 | tf_op jit(solution)/shard_map/sub | solution.py:112
  318.0 1.9 collective-permute-start.3
  319.9 2.6 slice.155
  322.5 3.1 slice.157
  325.7 5.9 %subtract_divide_fusion.6 = (f32[32,4,16,512]{3,0,2,1:T(8,128)S(1)}, f32[32,4,16,512]{3,0,2,1:T(8,128)S(1)}) fusion(f32[32,4,16,512]{3,0,2,1:T(8,128)S(1)} %get-tuple-element.16, f32[4]{0:T(128)S(1)} %broadcast_divide_fusion, f32[32,4,16,512]{3,0,2,1:T(8,128)S(1)} %fusion.4, f32[32,4,16,511]{3,0,2,1:T(8,128)} %slice.157, ...), kind=kLoop, calls=%fused_computation.49 | loop fusion | flops 16777216 | bytes 29352480 | tf_op jit(solution)/shard_map/div | solution.py:63
  331.6 2.8 collective-permute-start.4
  334.4 0.7 slice.159
  335.1 6.7 %collective-permute-done.4 = bf16[32,4,1,512]{3,0,2,1:T(8,128)(2,1)S(1)} collective-permute-done((bf16[32,4,1,512]{3,0,2,1:T(8,128)(2,1)S(1)}, bf16[32,4,1,512]{3,0,2,1:T(8,128)(2,1)S(1)}, u32[]{:S(2)}, u32[]{:S(2)}) %collective-permute-start.4) | collective-permute-done | bytes 131104 | tf_op jit(solution)/shard_map/ppermute | solution.py:22
  341.8 5.2 %fusion.8 = f32[32,4,16,512]{3,0,2,1:T(8,128)S(1)} fusion(f32[32,4,16,512]{3,0,2,1:T(8,128)S(1)} %get-tuple-element.15, f32[32,4,15,512]{3,0,2,1:T(8,128)S(1)} %slice.159, f32[32,4,1,512]{3,0,2,1:T(8,128)S(1)} %convert_element_type.98, f32[32,4,16,512]{3,0,2,1:T(8,128)S(1)} %get-tuple-element.14, f32[32,4,16,511]{3,0,2,1:T(8,128)S(1)} %bitcast.86, ...), kind=kLoop, calls=%fused_computation.17 | loop fusion | flops 11534336 | bytes 26206228 | tf_op jit(solution)/shard_map/sub | solution.py:112
  347.1 1.9 collective-permute-start.5
  349.0 2.6 slice.161
  351.6 3.1 slice.163
  354.7 5.9 %subtract_divide_fusion.4 = (f32[32,4,16,512]{3,0,2,1:T(8,128)S(1)}, f32[32,4,16,512]{3,0,2,1:T(8,128)S(1)}) fusion(f32[32,4,16,512]{3,0,2,1:T(8,128)S(1)} %get-tuple-element.14, f32[4]{0:T(128)S(1)} %broadcast_divide_fusion, f32[32,4,16,512]{3,0,2,1:T(8,128)S(1)} %fusion.8, f32[32,4,16,511]{3,0,2,1:T(8,128)} %slice.163, ...), kind=kLoop, calls=%fused_computation.45 | loop fusion | flops 16777216 | bytes 29352480 | tf_op jit(solution)/shard_map/div | solution.py:63
  360.6 2.4 collective-permute-start.6
  363.0 0.7 slice.165
  363.8 7.1 %collective-permute-done.6 = bf16[32,4,1,512]{3,0,2,1:T(8,128)(2,1)S(1)} collective-permute-done((bf16[32,4,1,512]{3,0,2,1:T(8,128)(2,1)S(1)}, bf16[32,4,1,512]{3,0,2,1:T(8,128)(2,1)S(1)}, u32[]{:S(2)}, u32[]{:S(2)}) %collective-permute-start.6) | collective-permute-done | bytes 131104 | tf_op jit(solution)/shard_map/ppermute | solution.py:22
  370.9 5.2 %fusion.12 = f32[32,4,16,512]{3,0,2,1:T(8,128)S(1)} fusion(f32[32,4,16,512]{3,0,2,1:T(8,128)S(1)} %get-tuple-element.13, f32[32,4,15,512]{3,0,2,1:T(8,128)S(1)} %slice.165, f32[32,4,1,512]{3,0,2,1:T(8,128)S(1)} %convert_element_type.100, f32[32,4,16,512]{3,0,2,1:T(8,128)S(1)} %get-tuple-element.12, f32[32,4,16,511]{3,0,2,1:T(8,128)S(1)} %bitcast.87, ...), kind=kLoop, calls=%fused_computation.23 | loop fusion | flops 11534336 | bytes 26206228 | tf_op jit(solution)/shard_map/sub | solution.py:112
  376.1 2.1 collective-permute-start.7
  378.2 2.6 slice.167
  380.8 3.1 slice.169
  383.9 5.9 %subtract_divide_fusion.2 = (f32[32,4,16,512]{3,0,2,1:T(8,128)S(1)}, f32[32,4,16,512]{3,0,2,1:T(8,128)S(1)}) fusion(f32[32,4,16,512]{3,0,2,1:T(8,128)S(1)} %get-tuple-element.12, f32[4]{0:T(128)S(1)} %broadcast_divide_fusion, f32[32,4,16,512]{3,0,2,1:T(8,128)S(1)} %fusion.12, f32[32,4,16,511]{3,0,2,1:T(8,128)} %slice.169, ...), kind=kLoop, calls=%fused_computation.41 | loop fusion | flops 16777216 | bytes 29352480 | tf_op jit(solution)/shard_map/div | solution.py:63
  389.8 2.4 collective-permute-start.8
  392.3 0.7 slice.171
  393.0 7.1 %collective-permute-done.8 = bf16[32,4,1,512]{3,0,2,1:T(8,128)(2,1)S(1)} collective-permute-done((bf16[32,4,1,512]{3,0,2,1:T(8,128)(2,1)S(1)}, bf16[32,4,1,512]{3,0,2,1:T(8,128)(2,1)S(1)}, u32[]{:S(2)}, u32[]{:S(2)}) %collective-permute-start.8) | collective-permute-done | bytes 131104 | tf_op jit(solution)/shard_map/ppermute | solution.py:22
  400.1 5.2 %fusion.16 = f32[32,4,16,512]{3,0,2,1:T(8,128)S(1)} fusion(f32[32,4,16,512]{3,0,2,1:T(8,128)S(1)} %get-tuple-element.11, f32[32,4,15,512]{3,0,2,1:T(8,128)S(1)} %slice.171, f32[32,4,1,512]{3,0,2,1:T(8,128)S(1)} %convert_element_type.102, f32[32,4,16,512]{3,0,2,1:T(8,128)S(1)} %get-tuple-element.10, f32[32,4,16,511]{3,0,2,1:T(8,128)S(1)} %bitcast.85, ...), kind=kLoop, calls=%fused_computation.29 | loop fusion | flops 11534336 | bytes 26206228 | tf_op jit(solution)/shard_map/sub | solution.py:112
  405.4 1.9 collective-permute-start.9
  407.3 2.6 slice.173
  409.9 3.1 slice.175
  413.0 5.9 %subtract_divide_fusion = (f32[32,4,16,512]{3,0,2,1:T(8,128)S(1)}, f32[32,4,16,512]{3,0,2,1:T(8,128)S(1)}) fusion(f32[32,4,16,512]{3,0,2,1:T(8,128)S(1)} %get-tuple-element.10, f32[4]{0:T(128)S(1)} %broadcast_divide_fusion, f32[32,4,16,512]{3,0,2,1:T(8,128)S(1)} %fusion.16, f32[32,4,16,511]{3,0,2,1:T(8,128)} %slice.175, ...), kind=kLoop, calls=%fused_computation.37 | loop fusion | flops 16777216 | bytes 29352480 | tf_op jit(solution)/shard_map/div | solution.py:63
  418.9 2.6 collective-permute-start.10
  421.5 0.7 slice.177
  422.3 5.0 %collective-permute-done.10 = bf16[32,4,1,512]{3,0,2,1:T(8,128)(2,1)S(1)} collective-permute-done((bf16[32,4,1,512]{3,0,2,1:T(8,128)(2,1)S(1)}, bf16[32,4,1,512]{3,0,2,1:T(8,128)(2,1)S(1)}, u32[]{:S(2)}, u32[]{:S(2)}) %collective-permute-start.10) | collective-permute-done | bytes 131104 | tf_op jit(solution)/shard_map/ppermute | solution.py:22
  427.3 5.1 %fusion.21 = bf16[32,4,16,512]{3,0,2,1:T(8,128)(2,1)S(1)} fusion(f32[32,4,16,512]{3,0,2,1:T(8,128)S(1)} %get-tuple-element.9, f32[32,4,15,512]{3,0,2,1:T(8,128)S(1)} %slice.177, f32[32,4,1,512]{3,0,2,1:T(8,128)S(1)} %convert_element_type.104, f32[32,4,16,512]{3,0,2,1:T(8,128)S(1)} %get-tuple-element.8, f32[32,4,16,511]{3,0,2,1:T(8,128)S(1)} %bitcast.89, ...), kind=kLoop, calls=%fused_computation.36 | loop fusion | flops 12582912 | bytes 24109076 | tf_op jit(solution)/shard_map/convert_element_type | solution.py:119
  432.5 2.5 copy.29
  (86 shorter events, 9.7 us)
Async XLA Ops:
  7.2 222.6 %copy-start = (f32[128,64]{0,1:T(8,128)S(1)}, f32[128,64]{0,1:T(8,128)}, u32[]{:S(2)}) copy-start(f32[128,64]{0,1:T(8,128)} %param.11) | copy-start | bytes 98308
  7.2 2.2 copy-start.2
  7.2 93.1 %all-gather.2.cloned.1.call-start = ((), (), s32[]{:S(2)}) async-start(), calls=%async_computation | async-start | bytes 10485760 | tf_op jit(solution)/shard_map/all_gather | solution.py:87
  7.2 2.5 copy-start.7
  13.3 4.2 copy-start.8
  15.5 271.5 %collective-permute-start = (bf16[32,4,1,512]{3,0,2,1:T(8,128)(2,1)}, bf16[32,4,1,512]{3,0,2,1:T(8,128)(2,1)S(1)}, u32[]{:S(2)}, u32[]{:S(2)}) collective-permute-start(bf16[32,4,1,512]{3,0,2,1:T(8,128)(2,1)} %convert_element_type.94), channel_id=1, source_target_pairs={{0,1},{1,2},{2,3},{3,4},{4,5},{5,6},{6,7},{7,8},{8,9},{9,10},{10,1... | collective-permute-start | bytes 393224 | tf_op jit(solution)/shard_map/ppermute | solution.py:22
  287.0 3.5 copy-start.3
  290.5 1.9 copy-start.5
  292.5 5.3 %collective-permute-start.1 = (bf16[32,4,1,512]{3,0,2,1:T(8,128)(2,1)S(1)}, bf16[32,4,1,512]{3,0,2,1:T(8,128)(2,1)S(1)}, u32[]{:S(2)}, u32[]{:S(2)}) collective-permute-start(bf16[32,4,1,512]{3,0,2,1:T(8,128)(2,1)S(1)} %slice.198), channel_id=1, source_target_pairs={{1,0},{2,1},{3,2},{4,3},{5,4},{6,5},{7,6},{8,7},{9,8},{10,9},{11,1... | collective-permute-start | bytes 393224 | tf_op jit(solution)/shard_map/ppermute | solution.py:22
  294.4 2.2 copy-start.6
  296.6 2.1 slice-start
  302.4 10.4 %copy-start.4 = (bf16[4,8,64,512]{3,2,1,0:T(8,128)(2,1)S(1)}, bf16[4,8,64,512]{3,2,1,0:T(8,128)(2,1)}, u32[]{:S(2)}) copy-start(bf16[4,8,64,512]{3,2,1,0:T(8,128)(2,1)} %copy-done.3) | copy-start | bytes 6291460
  302.4 10.4 %collective-permute-start.2 = (bf16[32,4,1,512]{3,0,2,1:T(8,128)(2,1)S(1)}, bf16[32,4,1,512]{3,0,2,1:T(8,128)(2,1)S(1)}, u32[]{:S(2)}, u32[]{:S(2)}) collective-permute-start(bf16[32,4,1,512]{3,0,2,1:T(8,128)(2,1)S(1)} %slice.197), channel_id=1, source_target_pairs={{0,1},{1,2},{2,3},{3,4},{4,5},{5,6},{6,7},{7,8},{8,9},{9,10},{10,1... | collective-permute-start | bytes 393224 | tf_op jit(solution)/shard_map/ppermute | solution.py:22
  318.0 7.6 %collective-permute-start.3 = (bf16[32,4,1,512]{3,0,2,1:T(8,128)(2,1)S(1)}, bf16[32,4,1,512]{3,0,2,1:T(8,128)(2,1)S(1)}, u32[]{:S(2)}, u32[]{:S(2)}) collective-permute-start(bf16[32,4,1,512]{3,0,2,1:T(8,128)(2,1)S(1)} %slice.196), channel_id=1, source_target_pairs={{1,0},{2,1},{3,2},{4,3},{5,4},{6,5},{7,6},{8,7},{9,8},{10,9},{11,1... | collective-permute-start | bytes 393224 | tf_op jit(solution)/shard_map/ppermute | solution.py:22
  331.6 10.2 %collective-permute-start.4 = (bf16[32,4,1,512]{3,0,2,1:T(8,128)(2,1)S(1)}, bf16[32,4,1,512]{3,0,2,1:T(8,128)(2,1)S(1)}, u32[]{:S(2)}, u32[]{:S(2)}) collective-permute-start(bf16[32,4,1,512]{3,0,2,1:T(8,128)(2,1)S(1)} %slice.195), channel_id=1, source_target_pairs={{0,1},{1,2},{2,3},{3,4},{4,5},{5,6},{6,7},{7,8},{8,9},{9,10},{10,1... | collective-permute-start | bytes 393224 | tf_op jit(solution)/shard_map/ppermute | solution.py:22
  347.1 7.6 %collective-permute-start.5 = (bf16[32,4,1,512]{3,0,2,1:T(8,128)(2,1)S(1)}, bf16[32,4,1,512]{3,0,2,1:T(8,128)(2,1)S(1)}, u32[]{:S(2)}, u32[]{:S(2)}) collective-permute-start(bf16[32,4,1,512]{3,0,2,1:T(8,128)(2,1)S(1)} %slice.194), channel_id=1, source_target_pairs={{1,0},{2,1},{3,2},{4,3},{5,4},{6,5},{7,6},{8,7},{9,8},{10,9},{11,1... | collective-permute-start | bytes 393224 | tf_op jit(solution)/shard_map/ppermute | solution.py:22
  360.6 10.2 %collective-permute-start.6 = (bf16[32,4,1,512]{3,0,2,1:T(8,128)(2,1)S(1)}, bf16[32,4,1,512]{3,0,2,1:T(8,128)(2,1)S(1)}, u32[]{:S(2)}, u32[]{:S(2)}) collective-permute-start(bf16[32,4,1,512]{3,0,2,1:T(8,128)(2,1)S(1)} %slice.193), channel_id=1, source_target_pairs={{0,1},{1,2},{2,3},{3,4},{4,5},{5,6},{6,7},{7,8},{8,9},{9,10},{10,1... | collective-permute-start | bytes 393224 | tf_op jit(solution)/shard_map/ppermute | solution.py:22
  376.1 7.8 %collective-permute-start.7 = (bf16[32,4,1,512]{3,0,2,1:T(8,128)(2,1)S(1)}, bf16[32,4,1,512]{3,0,2,1:T(8,128)(2,1)S(1)}, u32[]{:S(2)}, u32[]{:S(2)}) collective-permute-start(bf16[32,4,1,512]{3,0,2,1:T(8,128)(2,1)S(1)} %slice.192), channel_id=1, source_target_pairs={{1,0},{2,1},{3,2},{4,3},{5,4},{6,5},{7,6},{8,7},{9,8},{10,9},{11,1... | collective-permute-start | bytes 393224 | tf_op jit(solution)/shard_map/ppermute | solution.py:22
  389.8 10.2 %collective-permute-start.8 = (bf16[32,4,1,512]{3,0,2,1:T(8,128)(2,1)S(1)}, bf16[32,4,1,512]{3,0,2,1:T(8,128)(2,1)S(1)}, u32[]{:S(2)}, u32[]{:S(2)}) collective-permute-start(bf16[32,4,1,512]{3,0,2,1:T(8,128)(2,1)S(1)} %slice.191), channel_id=1, source_target_pairs={{0,1},{1,2},{2,3},{3,4},{4,5},{5,6},{6,7},{7,8},{8,9},{9,10},{10,1... | collective-permute-start | bytes 393224 | tf_op jit(solution)/shard_map/ppermute | solution.py:22
  405.4 7.6 %collective-permute-start.9 = (bf16[32,4,1,512]{3,0,2,1:T(8,128)(2,1)S(1)}, bf16[32,4,1,512]{3,0,2,1:T(8,128)(2,1)S(1)}, u32[]{:S(2)}, u32[]{:S(2)}) collective-permute-start(bf16[32,4,1,512]{3,0,2,1:T(8,128)(2,1)S(1)} %slice.190), channel_id=1, source_target_pairs={{1,0},{2,1},{3,2},{4,3},{5,4},{6,5},{7,6},{8,7},{9,8},{10,9},{11,1... | collective-permute-start | bytes 393224 | tf_op jit(solution)/shard_map/ppermute | solution.py:22
  418.9 8.4 %collective-permute-start.10 = (bf16[32,4,1,512]{3,0,2,1:T(8,128)(2,1)S(1)}, bf16[32,4,1,512]{3,0,2,1:T(8,128)(2,1)S(1)}, u32[]{:S(2)}, u32[]{:S(2)}) collective-permute-start(bf16[32,4,1,512]{3,0,2,1:T(8,128)(2,1)S(1)} %slice.189), channel_id=1, source_target_pairs={{0,1},{1,2},{2,3},{3,4},{4,5},{5,6},{6,7},{7,8},{8,9},{9,10},{10,1... | collective-permute-start | bytes 393224 | tf_op jit(solution)/shard_map/ppermute | solution.py:22
  427.3 7.6 %copy-start.1 = (f32[128,64]{0,1:T(8,128)S(1)}, f32[128,64]{0,1:T(8,128)}, u32[]{:S(2)}) copy-start(f32[128,64]{0,1:T(8,128)} %param.11) | copy-start | bytes 98308
Sparse Core Ops, SparseCore 0:
  15.0 85.3 all-gather.1
where the time goes:
time: 448 us; the launch traced here: 442 us
  blocking collectives  122 us (27%)
  waiting for transfers between devices  116 us (26%)
  other arithmetic  110 us (25%)
  local copies, waits for them, and re-layouts  39.3 us (9%)
  starting transfers between devices  24.5 us (5%)
  between operations  15 us (3%)
  matrix products  14.7 us (3%)
    psum x1, blocking collectives, local(): summed = lax.psum(block, 'pix')  110 us
    all_gather x1, waiting for transfers between devices, local(): everyone = lax.all_gather(flat, 'frame', axis=0, tiled=True)  82.8 us
    ppermute x11, waiting for transfers between devices, from_behind(): lax.ppermute(value, axis, [(source, source + steps) for source in range(l...  33 us
    div x5, other arithmetic, dual_update(): return ((first - step * down) / scale, (second - step * across) / scale)  27.1 us
    another operation x12, other arithmetic, mixing_matrix(): factor = jnp.linalg.cholesky(exact_dot(basis.T, image))  26.1 us
    ppermute x11, starting transfers between devices, from_behind(): lax.ppermute(value, axis, [(source, source + steps) for source in range(l...  24.5 us
    sub x5, other arithmetic, local(): smooth = source - lam * divergence(first, second)  24.3 us
    another operation x6, other arithmetic, mixing_matrix(): lax.linalg.triangular_solve(factor, image, left_side=False, lower=True, t...  16.6 us
  transfers between devices with their start and end apart: 12, of which 6 were waited for; matrix products, arithmetic and copies ran while one was open for 21% of the time, Pallas kernels for 0%

commit v1 on v0

--- a/solution.py
+++ b/solution.py
@@ -6,6 +6,12 @@
 POWER = 3
 NSWEEP = 5
 STEP_SIZE = 0.125
+
+
+def summed_here(x, mesh_axis):
+    pieces = lax.all_gather(x, mesh_axis, axis=0, tiled=False)
+    total = pieces.sum(axis=0)
+    return total
 
 
 def shortened(shard):
@@ -86,7 +92,7 @@
     flat = resid.reshape(count, chans * rows * cols)
     everyone = lax.all_gather(flat, "frame", axis=0, tiled=True)
     block = pair_rows(everyone, flat)
-    summed = lax.psum(block, "pix")
+    summed = summed_here(block, "pix")
     gram = lax.all_gather(summed, "frame", axis=1, tiled=True)
     gram = gram / nval
     mixing = mixing_matrix(gram, sketch)

time: 448 us -> 356 us (0.79)
  blocking collectives: 122 us -> 36.8 us
  waiting for transfers between devices: 116 us -> 108 us
    psum x1 -> x0, blocking collectives: 110 us -> none  [local(): summed = lax.psum(block, 'pix')]
    all_gather x0 -> x1, blocking collectives: none -> 24.8 us  [summed_here(): pieces = lax.all_gather(x, mesh_axis, axis=0, tiled=False)]
    ppermute x11, waiting for transfers between devices: 33 us -> 25.7 us  [from_behind(): lax.ppermute(value, axis, [(source, source + steps) for source in range(l...]
    unnamed x21 -> x22, local copies, waits for them, and re-layouts: 9.14 us -> 9.24 us
  transfers between devices with their start and end apart: 12 -> 12, of which waited for: 6 -> 6; matrix products, arithmetic and copies ran while one was open for 21% -> 26% of each run, Pallas kernels for 0% -> 0%
where the time goes in v1:
time: 356 us; the launch traced here: 349 us
  other arithmetic  110 us (31%)
  waiting for transfers between devices  108 us (30%)
  local copies, waits for them, and re-layouts  39.4 us (11%)
  blocking collectives  36.8 us (10%)
  starting transfers between devices  24.5 us (7%)
  between operations  15 us (4%)
  matrix products  14.7 us (4%)
    all_gather x1, waiting for transfers between devices, local(): everyone = lax.all_gather(flat, 'frame', axis=0, tiled=True)  82.8 us
    div x5, other arithmetic, dual_update(): return ((first - step * down) / scale, (second - step * across) / scale)  27.1 us
    another operation x12, other arithmetic, mixing_matrix(): factor = jnp.linalg.cholesky(exact_dot(basis.T, image))  26.1 us
    ppermute x11, waiting for transfers between devices, from_behind(): lax.ppermute(value, axis, [(source, source + steps) for source in range(l...  25.7 us
    all_gather x1, blocking collectives, summed_here(): pieces = lax.all_gather(x, mesh_axis, axis=0, tiled=False)  24.8 us
    ppermute x11, starting transfers between devices, from_behind(): lax.ppermute(value, axis, [(source, source + steps) for source in range(l...  24.5 us
    sub x5, other arithmetic, local(): smooth = source - lam * divergence(first, second)  24.3 us
    another operation x6, other arithmetic, mixing_matrix(): lax.linalg.triangular_solve(factor, image, left_side=False, lower=True, t...  16.6 us
  transfers between devices with their start and end apart: 12, of which 6 were waited for; matrix products, arithmetic and copies ran while one was open for 26% of the time, Pallas kernels for 0%

profile of v1, /device:TPU:8, one launch (start us, length us, event | category | flops | bytes accessed | tf_op | source)
XLA Modules:
  0.0 349.2 jit_solution(13859566698846477198)
XLA Ops:
  7.3 1.5 convert_element_type.88
  9.7 3.6 %fusion = bf16[32,4,16,512]{3,0,2,1:T(8,128)(2,1)S(1)} fusion(bf16[32,4,16,512]{3,2,1,0:T(8,128)(2,1)S(1)} %copy-done.7, f32[32,16,512]{2,0,1:T(8,128)S(1)} %copy.22, pred[4]{0:T(512)(128)(4,1)S(1)} %iota_compare_fusion.3, bf16[32,4,16,512]{3,2,1,0:T(8,128)(2,1)S(1)} %copy-done.2), kind=kLoop, calls=%fused_computation.5 | loop fusion | flops 6291456 | bytes 7340036 | tf_op jit(solution)/shard_map/convert_element_type | solution.py:89
  13.3 1.5 copy.30
  14.9 0.7 convert_element_type.94
  15.5 1.9 collective-permute-start
  17.5 82.8 %all-gather.3.cloned.1.call-done = bf16[128,32768]{1,0:T(8,128)(2,1)} async-done(((bf16[32,32768]{1,0:T(8,128)(2,1)}), bf16[128,32768]{1,0:T(8,128)(2,1)}) %all-gather.3.cloned.1.call-update) | async-done | bytes 8388624 | tf_op jit(solution)/shard_map/all_gather | solution.py:93
  100.3 6.9 %fusion.61 = f32[128,32]{0,1:T(8,128)S(1)} fusion(bf16[128,32768]{1,0:T(8,128)(2,1)} %all-gather.3.cloned.1.call-done, bf16[32,32768]{1,0:T(8,128)(2,1)} %bitcast.96), kind=kOutput, calls=%fused_computation.133 | convolution fusion | flops 268435456 | bytes 10502144 | tf_op jit(solution)/shard_map/dot_general | solution.py:55
  107.2 24.8 %all-gather = f32[4096,32]{0,1:T(8,128)S(1)} all-gather(f32[128,32]{0,1:T(8,128)S(1)} %fusion.61), channel_id=2, replica_groups=mesh['frame'=4,'pix'=32] {'pix'}, dimensions={0}, use_global_device_ids=true | all-gather | bytes 540672 | tf_op jit(solution)/shard_map/all_gather | solution.py:12
  132.1 12.0 %all_gather.15 = f32[128,128]{0,1:T(8,128)S(1)} all-gather(f32[128,32]{0,1:T(8,128)S(1)} %bitcast_reduce_fusion), channel_id=1, replica_groups=mesh['frame'=4,'pix'=32] {'frame'}, dimensions={1}, use_global_device_ids=true | all-gather | bytes 81920 | tf_op jit(solution)/shard_map/all_gather | solution.py:96
  144.7 5.8 %cholesky.74 = f32[64,64]{1,0:T(8,128)S(1)} custom-call(f32[64,64]{1,0:T(8,128)S(1)} %add_multiply_fusion), custom_call_target="Cholesky" | custom-call | tf_op jit(solution)/shard_map/jit(cholesky)/cholesky | solution.py:39
  151.2 0.7 fusion.32
  151.9 4.9 %custom-call.13 = f32[1,64,64]{1,2,0:T(8,128)S(1)} custom-call(f32[1,64,64]{2,1,0:T(8,128)S(1)} %fusion.32), custom_call_target="InvertDiagBlocksLowerTriangular" | custom-call | tf_op jit(solution)/shard_map/triangular_solve/custom-call.0 | solution.py:40
  157.5 5.8 %cholesky.85 = f32[64,64]{1,0:T(8,128)S(1)} custom-call(f32[64,64]{1,0:T(8,128)S(1)} %fusion.44), custom_call_target="Cholesky" | custom-call | tf_op jit(solution)/shard_map/jit(cholesky)/cholesky | solution.py:39
  164.7 4.9 %custom-call.14 = f32[1,64,64]{1,2,0:T(8,128)S(1)} custom-call(f32[1,64,64]{2,1,0:T(8,128)S(1)} %fusion.33), custom_call_target="InvertDiagBlocksLowerTriangular" | custom-call | tf_op jit(solution)/shard_map/triangular_solve/custom-call.0 | solution.py:40
  170.3 5.8 %cholesky.96 = f32[64,64]{1,0:T(8,128)S(1)} custom-call(f32[64,64]{1,0:T(8,128)S(1)} %fusion.42), custom_call_target="Cholesky" | custom-call | tf_op jit(solution)/shard_map/jit(cholesky)/cholesky | solution.py:39
  177.5 4.9 %custom-call.15 = f32[1,64,64]{1,2,0:T(8,128)S(1)} custom-call(f32[1,64,64]{2,1,0:T(8,128)S(1)} %fusion.34), custom_call_target="InvertDiagBlocksLowerTriangular" | custom-call | tf_op jit(solution)/shard_map/triangular_solve/custom-call.0 | solution.py:40
  183.4 5.8 %cholesky.107 = f32[64,64]{1,0:T(8,128)S(1)} custom-call(f32[64,64]{1,0:T(8,128)S(1)} %fusion.40), custom_call_target="Cholesky" | custom-call | tf_op jit(solution)/shard_map/jit(cholesky)/cholesky | solution.py:44
  190.6 4.9 %custom-call.10 = f32[1,64,64]{1,2,0:T(8,128)S(1)} custom-call(f32[1,64,64]{2,1,0:T(8,128)S(1)} %fusion.35), custom_call_target="InvertDiagBlocksLowerTriangular" | custom-call | tf_op jit(solution)/shard_map/triangular_solve | solution.py:48
  196.2 4.6 %convolution_convert_fusion = bf16[32,32768]{1,0:T(8,128)(2,1)S(1)} fusion(bf16[128,32768]{1,0:T(8,128)(2,1)} %all-gather.3.cloned.1.call-done, bf16[128,128]{0,1:T(8,128)(2,1)S(1)} %fusion.66, s32[]{:T(128)S(6)} %select_n.43), kind=kOutput, calls=%fused_computation | convolution fusion | flops 269484032 | bytes 10493956 | tf_op jit(solution)/shard_map/dot_general | solution.py:61
  200.8 0.7 copy.32
  201.6 3.5 multiply_subtract_fusion
  205.1 1.9 copy-done.5
  207.0 1.9 collective-permute-start.1
  208.9 2.2 copy-done.6
  211.1 1.1 slice.151
  212.3 0.9 slice-done
  213.2 3.6 %subtract_divide_fusion.8 = (f32[32,4,16,512]{3,0,2,1:T(8,128)S(1)}, f32[32,4,16,512]{3,0,2,1:T(8,128)S(1)}) fusion(f32[4]{0:T(128)S(1)} %broadcast_divide_fusion, f32[32,4,16,512]{3,0,2,1:T(8,128)S(1)} %copy-done.6, f32[32,4,16,511]{3,0,2,1:T(8,128)S(1)} %slice.151, pred[512]{0:T(512)(128)(4,1)S(1)} %iota_compare_fusion.2, ...), kind=kLoop, calls=%fused_computation.53 | loop fusion | flops 16777216 | bytes 20963872 | tf_op jit(solution)/shard_map/div | solution.py:69
  216.9 2.5 collective-permute-start.2
  219.4 0.7 slice.153
  220.1 5.3 %collective-permute-done.2 = bf16[32,4,1,512]{3,0,2,1:T(8,128)(2,1)S(1)} collective-permute-done((bf16[32,4,1,512]{3,0,2,1:T(8,128)(2,1)S(1)}, bf16[32,4,1,512]{3,0,2,1:T(8,128)(2,1)S(1)}, u32[]{:S(2)}, u32[]{:S(2)}) %collective-permute-start.2) | collective-permute-done | bytes 131104 | tf_op jit(solution)/shard_map/ppermute | solution.py:28
  225.4 5.2 %fusion.4 = f32[32,4,16,512]{3,0,2,1:T(8,128)S(1)} fusion(f32[32,4,16,512]{3,0,2,1:T(8,128)S(1)} %get-tuple-element.17, f32[32,4,15,512]{3,0,2,1:T(8,128)S(1)} %slice.153, f32[32,4,1,512]{3,0,2,1:T(8,128)S(1)} %convert_element_type.96, f32[32,4,16,512]{3,0,2,1:T(8,128)S(1)} %get-tuple-element.16, f32[32,4,16,511]{3,0,2,1:T(8,128)S(1)} %bitcast.93, ...), kind=kLoop, calls=%fused_computation.11 | loop fusion | flops 11534336 | bytes 26206228 | tf_op jit(solution)/shard_map/sub | solution.py:118
  230.7 1.9 collective-permute-start.3
  232.6 2.6 slice.155
  235.2 3.1 slice.157
  238.3 5.9 %subtract_divide_fusion.6 = (f32[32,4,16,512]{3,0,2,1:T(8,128)S(1)}, f32[32,4,16,512]{3,0,2,1:T(8,128)S(1)}) fusion(f32[32,4,16,512]{3,0,2,1:T(8,128)S(1)} %get-tuple-element.16, f32[4]{0:T(128)S(1)} %broadcast_divide_fusion, f32[32,4,16,512]{3,0,2,1:T(8,128)S(1)} %fusion.4, f32[32,4,16,511]{3,0,2,1:T(8,128)} %slice.157, ...), kind=kLoop, calls=%fused_computation.49 | loop fusion | flops 16777216 | bytes 29352480 | tf_op jit(solution)/shard_map/div | solution.py:69
  244.2 2.8 collective-permute-start.4
  247.0 0.7 slice.159
  247.8 4.8 %collective-permute-done.4 = bf16[32,4,1,512]{3,0,2,1:T(8,128)(2,1)S(1)} collective-permute-done((bf16[32,4,1,512]{3,0,2,1:T(8,128)(2,1)S(1)}, bf16[32,4,1,512]{3,0,2,1:T(8,128)(2,1)S(1)}, u32[]{:S(2)}, u32[]{:S(2)}) %collective-permute-start.4) | collective-permute-done | bytes 131104 | tf_op jit(solution)/shard_map/ppermute | solution.py:28
  252.6 5.2 %fusion.8 = f32[32,4,16,512]{3,0,2,1:T(8,128)S(1)} fusion(f32[32,4,16,512]{3,0,2,1:T(8,128)S(1)} %get-tuple-element.15, f32[32,4,15,512]{3,0,2,1:T(8,128)S(1)} %slice.159, f32[32,4,1,512]{3,0,2,1:T(8,128)S(1)} %convert_element_type.98, f32[32,4,16,512]{3,0,2,1:T(8,128)S(1)} %get-tuple-element.14, f32[32,4,16,511]{3,0,2,1:T(8,128)S(1)} %bitcast.91, ...), kind=kLoop, calls=%fused_computation.17 | loop fusion | flops 11534336 | bytes 26206228 | tf_op jit(solution)/shard_map/sub | solution.py:118
  257.9 1.9 collective-permute-start.5
  259.8 2.6 slice.161
  262.4 3.1 slice.163
  265.5 5.9 %subtract_divide_fusion.4 = (f32[32,4,16,512]{3,0,2,1:T(8,128)S(1)}, f32[32,4,16,512]{3,0,2,1:T(8,128)S(1)}) fusion(f32[32,4,16,512]{3,0,2,1:T(8,128)S(1)} %get-tuple-element.14, f32[4]{0:T(128)S(1)} %broadcast_divide_fusion, f32[32,4,16,512]{3,0,2,1:T(8,128)S(1)} %fusion.8, f32[32,4,16,511]{3,0,2,1:T(8,128)} %slice.163, ...), kind=kLoop, calls=%fused_computation.45 | loop fusion | flops 16777216 | bytes 29352480 | tf_op jit(solution)/shard_map/div | solution.py:69
  271.4 2.4 collective-permute-start.6
  273.8 0.7 slice.165
  274.6 5.3 %collective-permute-done.6 = bf16[32,4,1,512]{3,0,2,1:T(8,128)(2,1)S(1)} collective-permute-done((bf16[32,4,1,512]{3,0,2,1:T(8,128)(2,1)S(1)}, bf16[32,4,1,512]{3,0,2,1:T(8,128)(2,1)S(1)}, u32[]{:S(2)}, u32[]{:S(2)}) %collective-permute-start.6) | collective-permute-done | bytes 131104 | tf_op jit(solution)/shard_map/ppermute | solution.py:28
  279.9 5.2 %fusion.12 = f32[32,4,16,512]{3,0,2,1:T(8,128)S(1)} fusion(f32[32,4,16,512]{3,0,2,1:T(8,128)S(1)} %get-tuple-element.13, f32[32,4,15,512]{3,0,2,1:T(8,128)S(1)} %slice.165, f32[32,4,1,512]{3,0,2,1:T(8,128)S(1)} %convert_element_type.100, f32[32,4,16,512]{3,0,2,1:T(8,128)S(1)} %get-tuple-element.12, f32[32,4,16,511]{3,0,2,1:T(8,128)S(1)} %bitcast.92, ...), kind=kLoop, calls=%fused_computation.23 | loop fusion | flops 11534336 | bytes 26206228 | tf_op jit(solution)/shard_map/sub | solution.py:118
  285.1 2.1 collective-permute-start.7
  287.2 2.6 slice.167
  289.8 3.1 slice.169
  292.9 5.9 %subtract_divide_fusion.2 = (f32[32,4,16,512]{3,0,2,1:T(8,128)S(1)}, f32[32,4,16,512]{3,0,2,1:T(8,128)S(1)}) fusion(f32[32,4,16,512]{3,0,2,1:T(8,128)S(1)} %get-tuple-element.12, f32[4]{0:T(128)S(1)} %broadcast_divide_fusion, f32[32,4,16,512]{3,0,2,1:T(8,128)S(1)} %fusion.12, f32[32,4,16,511]{3,0,2,1:T(8,128)} %slice.169, ...), kind=kLoop, calls=%fused_computation.41 | loop fusion | flops 16777216 | bytes 29352480 | tf_op jit(solution)/shard_map/div | solution.py:69
  298.8 2.4 collective-permute-start.8
  301.2 0.7 slice.171
  302.0 5.3 %collective-permute-done.8 = bf16[32,4,1,512]{3,0,2,1:T(8,128)(2,1)S(1)} collective-permute-done((bf16[32,4,1,512]{3,0,2,1:T(8,128)(2,1)S(1)}, bf16[32,4,1,512]{3,0,2,1:T(8,128)(2,1)S(1)}, u32[]{:S(2)}, u32[]{:S(2)}) %collective-permute-start.8) | collective-permute-done | bytes 131104 | tf_op jit(solution)/shard_map/ppermute | solution.py:28
  307.2 5.2 %fusion.16 = f32[32,4,16,512]{3,0,2,1:T(8,128)S(1)} fusion(f32[32,4,16,512]{3,0,2,1:T(8,128)S(1)} %get-tuple-element.11, f32[32,4,15,512]{3,0,2,1:T(8,128)S(1)} %slice.171, f32[32,4,1,512]{3,0,2,1:T(8,128)S(1)} %convert_element_type.102, f32[32,4,16,512]{3,0,2,1:T(8,128)S(1)} %get-tuple-element.10, f32[32,4,16,511]{3,0,2,1:T(8,128)S(1)} %bitcast.90, ...), kind=kLoop, calls=%fused_computation.29 | loop fusion | flops 11534336 | bytes 26206228 | tf_op jit(solution)/shard_map/sub | solution.py:118
  312.5 1.9 collective-permute-start.9
  314.4 2.6 slice.173
  317.0 3.1 slice.175
  320.1 5.9 %subtract_divide_fusion = (f32[32,4,16,512]{3,0,2,1:T(8,128)S(1)}, f32[32,4,16,512]{3,0,2,1:T(8,128)S(1)}) fusion(f32[32,4,16,512]{3,0,2,1:T(8,128)S(1)} %get-tuple-element.10, f32[4]{0:T(128)S(1)} %broadcast_divide_fusion, f32[32,4,16,512]{3,0,2,1:T(8,128)S(1)} %fusion.16, f32[32,4,16,511]{3,0,2,1:T(8,128)} %slice.175, ...), kind=kLoop, calls=%fused_computation.37 | loop fusion | flops 16777216 | bytes 29352480 | tf_op jit(solution)/shard_map/div | solution.py:69
  326.0 2.6 collective-permute-start.10
  328.7 0.7 slice.177
  329.4 5.0 %collective-permute-done.10 = bf16[32,4,1,512]{3,0,2,1:T(8,128)(2,1)S(1)} collective-permute-done((bf16[32,4,1,512]{3,0,2,1:T(8,128)(2,1)S(1)}, bf16[32,4,1,512]{3,0,2,1:T(8,128)(2,1)S(1)}, u32[]{:S(2)}, u32[]{:S(2)}) %collective-permute-start.10) | collective-permute-done | bytes 131104 | tf_op jit(solution)/shard_map/ppermute | solution.py:28
  334.5 5.1 %fusion.21 = bf16[32,4,16,512]{3,0,2,1:T(8,128)(2,1)S(1)} fusion(f32[32,4,16,512]{3,0,2,1:T(8,128)S(1)} %get-tuple-element.9, f32[32,4,15,512]{3,0,2,1:T(8,128)S(1)} %slice.177, f32[32,4,1,512]{3,0,2,1:T(8,128)S(1)} %convert_element_type.104, f32[32,4,16,512]{3,0,2,1:T(8,128)S(1)} %get-tuple-element.8, f32[32,4,16,511]{3,0,2,1:T(8,128)S(1)} %bitcast.94, ...), kind=kLoop, calls=%fused_computation.36 | loop fusion | flops 12582912 | bytes 24109076 | tf_op jit(solution)/shard_map/convert_element_type | solution.py:125
  339.6 2.5 copy.29
  (88 shorter events, 9.8 us)
Async XLA Ops:
  7.2 137.0 %copy-start = (f32[128,64]{0,1:T(8,128)S(1)}, f32[128,64]{0,1:T(8,128)}, u32[]{:S(2)}) copy-start(f32[128,64]{0,1:T(8,128)} %param.11) | copy-start | bytes 98308
  7.2 2.2 copy-start.2
  7.2 93.1 %all-gather.3.cloned.1.call-start = ((), (), s32[]{:S(2)}) async-start(), calls=%async_computation | async-start | bytes 10485760 | tf_op jit(solution)/shard_map/all_gather | solution.py:93
  7.2 2.5 copy-start.7
  13.3 4.2 %copy-start.8 = (f32[4]{0:T(128)S(1)}, f32[4]{0:T(128)}, u32[]{:S(2)}) copy-start(f32[4]{0:T(128)} %param.12) | copy-start | bytes 52
  15.5 186.0 %collective-permute-start = (bf16[32,4,1,512]{3,0,2,1:T(8,128)(2,1)}, bf16[32,4,1,512]{3,0,2,1:T(8,128)(2,1)S(1)}, u32[]{:S(2)}, u32[]{:S(2)}) collective-permute-start(bf16[32,4,1,512]{3,0,2,1:T(8,128)(2,1)} %convert_element_type.94), channel_id=1, source_target_pairs={{0,1},{1,2},{2,3},{3,4},{4,5},{5,6},{6,7},{7,8},{8,9},{9,10},{10,1... | collective-permute-start | bytes 393224 | tf_op jit(solution)/shard_map/ppermute | solution.py:28
  201.5 3.5 copy-start.3
  205.0 1.9 copy-start.5
  207.0 5.3 %collective-permute-start.1 = (bf16[32,4,1,512]{3,0,2,1:T(8,128)(2,1)S(1)}, bf16[32,4,1,512]{3,0,2,1:T(8,128)(2,1)S(1)}, u32[]{:S(2)}, u32[]{:S(2)}) collective-permute-start(bf16[32,4,1,512]{3,0,2,1:T(8,128)(2,1)S(1)} %slice.198), channel_id=1, source_target_pairs={{1,0},{2,1},{3,2},{4,3},{5,4},{6,5},{7,6},{8,7},{9,8},{10,9},{11,1... | collective-permute-start | bytes 393224 | tf_op jit(solution)/shard_map/ppermute | solution.py:28
  208.9 2.2 copy-start.6
  211.1 2.1 slice-start
  216.8 8.6 %copy-start.4 = (bf16[4,8,64,512]{3,2,1,0:T(8,128)(2,1)S(1)}, bf16[4,8,64,512]{3,2,1,0:T(8,128)(2,1)}, u32[]{:S(2)}) copy-start(bf16[4,8,64,512]{3,2,1,0:T(8,128)(2,1)} %copy-done.3) | copy-start | bytes 6291460
  216.9 8.5 %collective-permute-start.2 = (bf16[32,4,1,512]{3,0,2,1:T(8,128)(2,1)S(1)}, bf16[32,4,1,512]{3,0,2,1:T(8,128)(2,1)S(1)}, u32[]{:S(2)}, u32[]{:S(2)}) collective-permute-start(bf16[32,4,1,512]{3,0,2,1:T(8,128)(2,1)S(1)} %slice.197), channel_id=1, source_target_pairs={{0,1},{1,2},{2,3},{3,4},{4,5},{5,6},{6,7},{7,8},{8,9},{9,10},{10,1... | collective-permute-start | bytes 393224 | tf_op jit(solution)/shard_map/ppermute | solution.py:28
  230.7 7.6 %collective-permute-start.3 = (bf16[32,4,1,512]{3,0,2,1:T(8,128)(2,1)S(1)}, bf16[32,4,1,512]{3,0,2,1:T(8,128)(2,1)S(1)}, u32[]{:S(2)}, u32[]{:S(2)}) collective-permute-start(bf16[32,4,1,512]{3,0,2,1:T(8,128)(2,1)S(1)} %slice.196), channel_id=1, source_target_pairs={{1,0},{2,1},{3,2},{4,3},{5,4},{6,5},{7,6},{8,7},{9,8},{10,9},{11,1... | collective-permute-start | bytes 393224 | tf_op jit(solution)/shard_map/ppermute | solution.py:28
  244.2 8.4 %collective-permute-start.4 = (bf16[32,4,1,512]{3,0,2,1:T(8,128)(2,1)S(1)}, bf16[32,4,1,512]{3,0,2,1:T(8,128)(2,1)S(1)}, u32[]{:S(2)}, u32[]{:S(2)}) collective-permute-start(bf16[32,4,1,512]{3,0,2,1:T(8,128)(2,1)S(1)} %slice.195), channel_id=1, source_target_pairs={{0,1},{1,2},{2,3},{3,4},{4,5},{5,6},{6,7},{7,8},{8,9},{9,10},{10,1... | collective-permute-start | bytes 393224 | tf_op jit(solution)/shard_map/ppermute | solution.py:28
  257.9 7.6 %collective-permute-start.5 = (bf16[32,4,1,512]{3,0,2,1:T(8,128)(2,1)S(1)}, bf16[32,4,1,512]{3,0,2,1:T(8,128)(2,1)S(1)}, u32[]{:S(2)}, u32[]{:S(2)}) collective-permute-start(bf16[32,4,1,512]{3,0,2,1:T(8,128)(2,1)S(1)} %slice.194), channel_id=1, source_target_pairs={{1,0},{2,1},{3,2},{4,3},{5,4},{6,5},{7,6},{8,7},{9,8},{10,9},{11,1... | collective-permute-start | bytes 393224 | tf_op jit(solution)/shard_map/ppermute | solution.py:28
  271.4 8.4 %collective-permute-start.6 = (bf16[32,4,1,512]{3,0,2,1:T(8,128)(2,1)S(1)}, bf16[32,4,1,512]{3,0,2,1:T(8,128)(2,1)S(1)}, u32[]{:S(2)}, u32[]{:S(2)}) collective-permute-start(bf16[32,4,1,512]{3,0,2,1:T(8,128)(2,1)S(1)} %slice.193), channel_id=1, source_target_pairs={{0,1},{1,2},{2,3},{3,4},{4,5},{5,6},{6,7},{7,8},{8,9},{9,10},{10,1... | collective-permute-start | bytes 393224 | tf_op jit(solution)/shard_map/ppermute | solution.py:28
  285.1 7.8 %collective-permute-start.7 = (bf16[32,4,1,512]{3,0,2,1:T(8,128)(2,1)S(1)}, bf16[32,4,1,512]{3,0,2,1:T(8,128)(2,1)S(1)}, u32[]{:S(2)}, u32[]{:S(2)}) collective-permute-start(bf16[32,4,1,512]{3,0,2,1:T(8,128)(2,1)S(1)} %slice.192), channel_id=1, source_target_pairs={{1,0},{2,1},{3,2},{4,3},{5,4},{6,5},{7,6},{8,7},{9,8},{10,9},{11,1... | collective-permute-start | bytes 393224 | tf_op jit(solution)/shard_map/ppermute | solution.py:28
  298.8 8.4 %collective-permute-start.8 = (bf16[32,4,1,512]{3,0,2,1:T(8,128)(2,1)S(1)}, bf16[32,4,1,512]{3,0,2,1:T(8,128)(2,1)S(1)}, u32[]{:S(2)}, u32[]{:S(2)}) collective-permute-start(bf16[32,4,1,512]{3,0,2,1:T(8,128)(2,1)S(1)} %slice.191), channel_id=1, source_target_pairs={{0,1},{1,2},{2,3},{3,4},{4,5},{5,6},{6,7},{7,8},{8,9},{9,10},{10,1... | collective-permute-start | bytes 393224 | tf_op jit(solution)/shard_map/ppermute | solution.py:28
  312.5 7.6 %collective-permute-start.9 = (bf16[32,4,1,512]{3,0,2,1:T(8,128)(2,1)S(1)}, bf16[32,4,1,512]{3,0,2,1:T(8,128)(2,1)S(1)}, u32[]{:S(2)}, u32[]{:S(2)}) collective-permute-start(bf16[32,4,1,512]{3,0,2,1:T(8,128)(2,1)S(1)} %slice.190), channel_id=1, source_target_pairs={{1,0},{2,1},{3,2},{4,3},{5,4},{6,5},{7,6},{8,7},{9,8},{10,9},{11,1... | collective-permute-start | bytes 393224 | tf_op jit(solution)/shard_map/ppermute | solution.py:28
  326.0 8.4 %collective-permute-start.10 = (bf16[32,4,1,512]{3,0,2,1:T(8,128)(2,1)S(1)}, bf16[32,4,1,512]{3,0,2,1:T(8,128)(2,1)S(1)}, u32[]{:S(2)}, u32[]{:S(2)}) collective-permute-start(bf16[32,4,1,512]{3,0,2,1:T(8,128)(2,1)S(1)} %slice.189), channel_id=1, source_target_pairs={{0,1},{1,2},{2,3},{3,4},{4,5},{5,6},{6,7},{7,8},{8,9},{9,10},{10,1... | collective-permute-start | bytes 393224 | tf_op jit(solution)/shard_map/ppermute | solution.py:28
  334.5 7.6 %copy-start.1 = (f32[128,64]{0,1:T(8,128)S(1)}, f32[128,64]{0,1:T(8,128)}, u32[]{:S(2)}) copy-start(f32[128,64]{0,1:T(8,128)} %param.11) | copy-start | bytes 98308
Sparse Core Ops, SparseCore 0:
  15.0 85.3 all-gather.2
